TPU v7x, 512 devices: a whole 4x8x8 slice. The times are simulated.
512 devices in a mesh: clip: 16 (over y_lo, z), seq: 32 (over x, y_hi, core).
Axes of the slice: x: 4, y: 8 (y_hi: 4, y_lo: 2; y = y_hi * 2 + y_lo), z: 8, core: 2. Of those that a mesh axis runs over, the one named last changes fastest.
Arguments:
- patches: bfloat16 [16, 6272, 1024], P('clip', 'seq'), may hold values from -6 to 12
- segment: int32 [16, 6272], P('clip', 'seq'), may hold values from 0 to 191, as said below
- dest_shard: int32 [16, 6144], P('clip', 'seq'), may hold values from -1 to 31, as said below
- dest_slot: int32 [16, 6144], P('clip', 'seq'), may hold values from -1 to 63, as said below
- w_qkv: bfloat16 [1024, 1536], replicated, may hold values from -1 to 4
- out_grad: bfloat16 [16, 2048, 512], P('clip', 'seq'), may hold values from -6 to 6
Outputs:
- attended: bfloat16 [16, 2048, 512], P('clip', 'seq')
- patch_grad: bfloat16 [16, 6272, 1024], P('clip', 'seq')
- weight_grad: float32 [1024, 1536], P('seq', 'clip')
Inputs may be any that keep to these rules, and one draw needn't show every extreme that they name: `segment`: within each block of 196 patches the ids start at 0, never fall and skip no value; every id names one or more patches. The number of tokens of a block is one more than its largest id. `dest_shard`: -1 exactly on the rows of a block past its number of tokens. A block of 192 rows sends at most 6 rows to each receiving block of its clip, and every receiving block gets exactly 64 rows. `dest_slot`: -1 exactly where dest_shard is -1; the rows sent to one receiving block take its rows 0 to 63 once each.
All inputs are finite; a program needn't handle non-finite values.
Results may differ from a plain program's by a relative error of at most 0.024.
Values may be sent and summed in bfloat16 or wider, within the bound.
A program may use at most 64 MiB of HBM per device.

v0:
```python
import jax
import jax.numpy as jnp
from jax import lax
from jax.sharding import PartitionSpec as P

HEADS = 8
HEAD_DIM = 64
neg_large = -1e30


def split_heads(rows_in):
    return rows_in.reshape(rows_in.shape[0], HEADS, HEAD_DIM)


def forward_fold(query_heads, running, pieces):
    scaling = HEAD_DIM ** (-0.5)
    row_max, row_total, weighted = running
    key_heads = split_heads(pieces[0])
    value_heads = split_heads(pieces[1])
    scores = (
        jnp.einsum("rhd,khd->hrk", query_heads, key_heads, preferred_element_type=jnp.float32)
        * scaling
    )
    new_max = jnp.maximum(row_max, jnp.max(scores, axis=2))
    weights = jnp.exp(scores - new_max[:, :, None])
    row_total = jnp.sum(weights, axis=2)
    weighted = jnp.einsum(
        "hrk,khd->hrd",
        weights.astype(jnp.bfloat16),
        value_heads,
        preferred_element_type=jnp.float32,
    )
    return (new_max, row_total, weighted)


def query_fold(query_heads, grad_heads, log_total, grad_dot):
    scaling = HEAD_DIM ** (-0.5)

    def combine_piece(running, pieces, offset):
        key_heads = split_heads(pieces[0])
        value_heads = split_heads(pieces[1])
        scores = (
            jnp.einsum("rhd,khd->hrk", query_heads, key_heads, preferred_element_type=jnp.float32)
            * scaling
        )
        probability = jnp.exp(scores - log_total[:, :, None])
        prob_grad = jnp.einsum(
            "rhd,khd->hrk", grad_heads, value_heads, preferred_element_type=jnp.float32
        )
        score_grad = (probability * (prob_grad - grad_dot[:, :, None])).astype(jnp.bfloat16)
        return (
            jnp.einsum("hrk,khd->hrd", score_grad, key_heads, preferred_element_type=jnp.float32)
            * scaling
        )

    return combine_piece


def key_fold(key_heads, value_heads, all_log, all_dot, pieces):
    scaling = HEAD_DIM ** (-0.5)
    piece_query = split_heads(pieces[0])
    piece_grad = split_heads(pieces[1])
    piece_log = all_log.T
    piece_dot = all_dot.T
    scores = (
        jnp.einsum("qhd,khd->hqk", piece_query, key_heads, preferred_element_type=jnp.float32)
        * scaling
    )
    probability = jnp.exp(scores - piece_log[:, :, None])
    value_grad = jnp.einsum(
        "hqk,qhd->hkd",
        probability.astype(jnp.bfloat16),
        piece_grad,
        preferred_element_type=jnp.float32,
    )
    prob_grad = jnp.einsum(
        "qhd,khd->hqk", piece_grad, value_heads, preferred_element_type=jnp.float32
    )
    score_grad = (probability * (prob_grad - piece_dot[:, :, None])).astype(jnp.bfloat16)
    key_grad = (
        jnp.einsum("hqk,qhd->hkd", score_grad, piece_query, preferred_element_type=jnp.float32)
        * scaling
    )
    return (key_grad, value_grad)


def head_rows(matrix):
    return matrix.transpose(1, 0, 2).reshape(matrix.shape[1], HEADS * HEAD_DIM)


def local(patches, segment, dest_shard, dest_slot, w_qkv, out_grad):
    shard_count = lax.axis_size("seq")
    patch_rows = patches[0]
    patch_token = segment[0]
    targets = dest_shard[0]
    slot_ids = dest_slot[0]
    token_cap = targets.shape[0]
    pair_cap = token_cap // shard_count
    local_rows = out_grad.shape[1]
    inner_width = HEADS * HEAD_DIM
    member = (
        lax.broadcasted_iota(jnp.int32, (token_cap, patch_token.shape[0]), 0)
        == patch_token[None, :]
    )
    member_half = member.astype(jnp.bfloat16)
    counts = jnp.sum(member.astype(jnp.float32), axis=1)
    token_sums = jnp.dot(member_half, patch_rows, preferred_element_type=jnp.float32)
    tokens = (token_sums / jnp.maximum(counts, 1.0)[:, None]).astype(jnp.bfloat16)
    to_shard = (
        targets[:, None] == lax.broadcasted_iota(jnp.int32, (token_cap, shard_count), 1)
    ).astype(jnp.int32)
    ranking = jnp.sum((jnp.cumsum(to_shard, axis=0) - 1) * to_shard, axis=1)
    position = jnp.where(targets >= 0, targets * pair_cap + ranking, -1)
    chooser = position[None, :] == lax.broadcasted_iota(
        jnp.int32, (shard_count * pair_cap, token_cap), 0
    )
    chooser_half = chooser.astype(jnp.bfloat16)
    send_rows = jnp.dot(chooser_half, tokens, preferred_element_type=jnp.float32).astype(
        jnp.bfloat16
    )
    send_slot = jnp.sum(chooser.astype(jnp.int32) * (slot_ids + 1)[None, :], axis=1) - 1
    came_rows, came_slot = (
        lax.all_to_all(
            send_rows.reshape(shard_count, pair_cap, -1),
            "seq",
            split_axis=0,
            concat_axis=0,
            tiled=True,
        ),
        lax.all_to_all(
            send_slot.reshape(shard_count, pair_cap), "seq", split_axis=0, concat_axis=0, tiled=True
        ),
    )
    came_slot = came_slot.reshape(-1)
    placer = (
        came_slot[None, :]
        == lax.broadcasted_iota(jnp.int32, (local_rows, shard_count * pair_cap), 0)
    ).astype(jnp.bfloat16)
    placed = jnp.dot(
        placer, came_rows.reshape(shard_count * pair_cap, -1), preferred_element_type=jnp.float32
    ).astype(jnp.bfloat16)
    projected = jnp.dot(placed, w_qkv, preferred_element_type=jnp.float32).astype(jnp.bfloat16)
    query_rows = projected[:, :inner_width]
    key_rows = projected[:, inner_width : 2 * inner_width]
    value_rows = projected[:, 2 * inner_width :]
    query_heads = split_heads(query_rows)
    initial = (
        jnp.full((HEADS, local_rows), neg_large, jnp.float32),
        jnp.zeros((HEADS, local_rows), jnp.float32),
        jnp.zeros((HEADS, local_rows, HEAD_DIM), jnp.float32),
    )
    row_max, row_total, weighted = forward_fold(
        query_heads,
        initial,
        (
            lax.all_gather(key_rows, "seq", axis=0, tiled=True),
            lax.all_gather(value_rows, "seq", axis=0, tiled=True),
        ),
    )
    attended_rows = head_rows((weighted / row_total[:, :, None]).astype(jnp.bfloat16))
    grad_rows = out_grad[0]
    grad_heads = split_heads(grad_rows)
    log_total = row_max + jnp.log(row_total)
    grad_dot = jnp.sum(
        grad_heads.astype(jnp.float32) * split_heads(attended_rows).astype(jnp.float32), axis=2
    )
    blank = jnp.zeros((HEADS, local_rows, HEAD_DIM), jnp.float32)
    query_step = query_fold(query_heads, grad_heads, log_total, grad_dot.T)
    query_grad = query_step(
        blank,
        (
            lax.all_gather(key_rows, "seq", axis=0, tiled=True),
            lax.all_gather(value_rows, "seq", axis=0, tiled=True),
        ),
        jnp.int32(0),
    )
    all_log, all_dot = (
        lax.all_gather(log_total.T, "seq", axis=0, tiled=True),
        lax.all_gather(grad_dot, "seq", axis=0, tiled=True),
    )
    key_grad, value_grad = key_fold(
        split_heads(key_rows),
        split_heads(value_rows),
        all_log,
        all_dot,
        (
            lax.all_gather(query_rows, "seq", axis=0, tiled=True),
            lax.all_gather(grad_rows, "seq", axis=0, tiled=True),
        ),
    )
    proj_grad = jnp.concatenate(
        [head_rows(query_grad), head_rows(key_grad), head_rows(value_grad)], axis=1
    ).astype(jnp.bfloat16)
    placed_grad = jnp.einsum(
        "rc,dc->rd", proj_grad, w_qkv, preferred_element_type=jnp.float32
    ).astype(jnp.bfloat16)
    partial_value = jnp.einsum(
        "rd,rc->dc", placed, proj_grad, preferred_element_type=jnp.float32
    ).astype(jnp.bfloat16)
    across = lax.psum_scatter(partial_value, "seq", scatter_dimension=0, tiled=True).astype(
        jnp.float32
    )
    weight_grad = lax.psum_scatter(
        across.astype(jnp.bfloat16), "clip", scatter_dimension=1, tiled=True
    ).astype(jnp.float32)
    back_rows = jnp.einsum(
        "rj,rd->jd", placer, placed_grad, preferred_element_type=jnp.float32
    ).astype(jnp.bfloat16)
    returned = lax.all_to_all(
        back_rows.reshape(shard_count, pair_cap, -1), "seq", split_axis=0, concat_axis=0, tiled=True
    )
    token_grad = jnp.einsum(
        "jt,jd->td",
        chooser_half,
        returned.reshape(shard_count * pair_cap, -1),
        preferred_element_type=jnp.float32,
    ).astype(jnp.bfloat16)
    patch_sums = jnp.einsum(
        "tp,td->pd", member_half, token_grad, preferred_element_type=jnp.float32
    )
    patch_count = jnp.sum(member.astype(jnp.float32) * counts[:, None], axis=0)
    patch_grad = (patch_sums / patch_count[:, None]).astype(jnp.bfloat16)
    return (attended_rows[None], patch_grad[None], weight_grad)


def solution(mesh):
    return jax.shard_map(
        local,
        mesh=mesh,
        in_specs=(
            P("clip", "seq", None),
            P("clip", "seq"),
            P("clip", "seq"),
            P("clip", "seq"),
            P(),
            P("clip", "seq", None),
        ),
        out_specs=(P("clip", "seq", None), P("clip", "seq", None), P("seq", "clip")),
        check_vma=False,
    )
```

profile of v0, /device:TPU:2, one launch (start us, length us, event | category | flops | bytes accessed | tf_op | source)
XLA Modules:
  0.0 507.5 jit_solution(14821409125250477801)
XLA Ops:
  13.2 10.3 %all-to-all-start = ((s32[32,1,6]{2,1,0:T(1,128)}), s32[32,1,6]{2,1,0:T(1,128)S(1)}, u32[]{:S(2)}, u32[]{:S(2)}) async-start(s32[32,1,6]{2,1,0:T(1,128)} %bitcast.5), calls=%async_computation | async-start | bytes 32768 | tf_op jit(solution)/shard_map/all_to_all | solution.py:130
  27.9 4.2 all-to-all-done
  32.0 5.7 %all-to-all-start.1 = ((bf16[32,6,1024]{2,1,0:T(8,128)(2,1)}), bf16[32,6,1024]{2,1,0:T(8,128)(2,1)}, u32[]{:S(2)}, u32[]{:S(2)}) async-start(bf16[32,6,1024]{2,1,0:T(8,128)(2,1)} %reshape.104), calls=%async_computation.1 | async-start | bytes 1048576 | tf_op jit(solution)/shard_map/all_to_all | solution.py:123
  39.1 15.6 %all-to-all-done.1 = bf16[32,6,1024]{2,1,0:T(8,128)(2,1)} async-done(((bf16[32,6,1024]{2,1,0:T(8,128)(2,1)}), bf16[32,6,1024]{2,1,0:T(8,128)(2,1)}, u32[]{:S(2)}, u32[]{:S(2)}) %all-to-all-start.1) | async-done | bytes 393248 | tf_op jit(solution)/shard_map/all_to_all | solution.py:123
  63.8 13.4 %all-gather.14.cloned.1.call-done = bf16[1,2048,512]{2,1,0:T(8,128)(2,1)} async-done(((bf16[1,64,512]{2,1,0:T(8,128)(2,1)}), bf16[1,2048,512]{2,1,0:T(8,128)(2,1)}) %all-gather.14.cloned.1.call-update) | async-done | bytes 2097168 | tf_op jit(solution)/shard_map/all_gather | solution.py:188
  77.3 3.9 copy.62
  81.2 56.0 %all-gather.8.cloned.1.call-done = bf16[2048,512]{1,0:T(8,128)(2,1)} async-done(((bf16[64,512]{1,0:T(8,128)(2,1)}), bf16[2048,512]{1,0:T(8,128)(2,1)}) %all-gather.8.cloned.1.call-update) | async-done | bytes 2097168 | tf_op jit(solution)/shard_map/all_gather | solution.py:156
  137.3 3.9 copy.53
  141.2 56.1 %all-gather.10.cloned.1.call-done = bf16[2048,512]{1,0:T(8,128)(2,1)} async-done(((bf16[64,512]{1,0:T(8,128)(2,1)}), bf16[2048,512]{1,0:T(8,128)(2,1)}) %all-gather.10.cloned.1.call-update) | async-done | bytes 2097168 | tf_op jit(solution)/shard_map/all_gather | solution.py:157
  197.3 4.0 copy.55
  201.2 2.4 multiply_reduce_fusion
  208.3 5.2 %fusion.28 = bf16[64,8,64]{2,0,1:T(8,128)(2,1)S(1)} fusion(bf16[2048,8,64]{0,2,1:T(8,128)(2,1)} %bitcast.106, f32[8,64,2048]{2,1,0:T(8,128)} %copy-done.1, bf16[2048,8,64]{0,2,1:T(8,128)(2,1)} %bitcast.107, bf16[64,8,64]{0,2,1:T(8,128)(2,1)S(1)} %bitcast.114, f32[8,64]{1,0:T(8,128)S(1)} %bitcast.120, f32[8,64]{1,0:T(8,128)} %log_add_fusion), kind=kOutput, calls=%fused_computation.36 | convolution fusion | flops 273743872 | bytes 8523776 | tf_op jit(solution)/shard_map/hrk,khd->hrd/dot_general | solution.py:52
  214.5 38.9 %all-gather.2 = f32[32,64,8]{1,2,0:T(8,128)S(1)} all-gather(f32[1,64,8]{1,2,0:T(8,128)S(1)} %bitcast.121), channel_id=1, replica_groups=mesh['clip'=16,'seq'=32] {'seq'}, dimensions={0}, use_global_device_ids=true | all-gather | bytes 67584 | tf_op jit(solution)/shard_map/all_gather | solution.py:179
  254.2 40.2 %all-gather.1 = f32[32,64,8]{1,2,0:T(8,128)S(1)} all-gather(f32[1,64,8]{1,2,0:T(8,128)S(1)} %fusion.58), channel_id=1, replica_groups=mesh['clip'=16,'seq'=32] {'seq'}, dimensions={0}, use_global_device_ids=true | all-gather | bytes 67584 | tf_op jit(solution)/shard_map/all_gather | solution.py:178
  295.4 4.0 copy.59
  299.3 2.4 fusion.44
  301.8 2.0 fusion.30
  303.8 5.9 %fusion.29 = bf16[64,8,64]{2,0,1:T(8,128)(2,1)} fusion(bf16[2048,8,64]{0,2,1:T(8,128)(2,1)} %bitcast.104, f32[8,2048,64]{1,2,0:T(8,128)} %copy-done.2, bf16[2048,8,64]{0,2,1:T(8,128)(2,1)} %bitcast.101, f32[8,2048]{1,0:T(8,128)} %bitcast.115, f32[8,2048]{1,0:T(8,128)S(1)} %bitcast.111, bf16[64,8,64]{2,1,0:T(8,128)(2,1)} %reshape.112), kind=kOutput, calls=%fused_computation.37 | convolution fusion | flops 273743872 | bytes 8650752 | tf_op jit(solution)/shard_map/hqk,qhd->hkd/dot_general | solution.py:81
  316.5 2.6 convolution_convert_fusion
  319.2 2.2 convolution_convert_fusion.3
  322.3 10.2 %all-to-all-start.2 = ((bf16[32,6,1024]{2,1,0:T(8,128)(2,1)}), bf16[32,6,1024]{2,1,0:T(8,128)(2,1)}, u32[]{:S(2)}, u32[]{:S(2)}) async-start(bf16[32,6,1024]{2,1,0:T(8,128)(2,1)} %reshape.116), calls=%async_computation.2 | async-start | bytes 1048576 | tf_op jit(solution)/shard_map/all_to_all | solution.py:209
  334.4 13.7 %all-to-all-done.2 = bf16[32,6,1024]{2,1,0:T(8,128)(2,1)} async-done(((bf16[32,6,1024]{2,1,0:T(8,128)(2,1)}), bf16[32,6,1024]{2,1,0:T(8,128)(2,1)}, u32[]{:S(2)}, u32[]{:S(2)}) %all-to-all-start.2) | async-done | bytes 393248 | tf_op jit(solution)/shard_map/all_to_all | solution.py:209
  349.2 74.2 %reduce-scatter.5.cloned.1.call-done = bf16[32,1536]{1,0:T(8,128)(2,1)} async-done(((bf16[1024,1536]{1,0:T(8,128)(2,1)}), bf16[32,1536]{1,0:T(8,128)(2,1)}) %reduce-scatter.5.cloned.1.call-update) | async-done | bytes 98320 | tf_op jit(solution)/shard_map/reduce_scatter | solution.py:200
  426.5 72.7 %reduce-scatter.7.cloned.1.call-done = bf16[96,32]{1,0:T(8,128)(2,1)} async-done(((bf16[1536,32]{1,0:T(8,128)(2,1)}), bf16[96,32]{1,0:T(8,128)(2,1)}) %reduce-scatter.7.cloned.1.call-update) | async-done | bytes 6160
  (97 shorter events, 43.4 us)
Async XLA Ops:
  7.2 49.6 %copy-start = (bf16[1024,1536]{1,0:T(8,128)(2,1)S(1)}, bf16[1024,1536]{1,0:T(8,128)(2,1)}, u32[]{:S(2)}) copy-start(bf16[1024,1536]{1,0:T(8,128)(2,1)} %param.10) | copy-start | bytes 9437188
  7.2 70.1 %all-gather.14.cloned.1.call-start = ((), (), s32[]{:S(2)}) async-start(), calls=%async_computation.9 | async-start | bytes 2162688 | tf_op jit(solution)/shard_map/all_gather | solution.py:188
  11.8 0.6 copy-start.12
  13.2 18.8 %all-to-all-start = ((s32[32,1,6]{2,1,0:T(1,128)}), s32[32,1,6]{2,1,0:T(1,128)S(1)}, u32[]{:S(2)}, u32[]{:S(2)}) async-start(s32[32,1,6]{2,1,0:T(1,128)} %bitcast.5), calls=%async_computation | async-start | bytes 32768 | tf_op jit(solution)/shard_map/all_to_all | solution.py:130
  24.3 0.6 copy-start.10
  32.0 22.7 %all-to-all-start.1 = ((bf16[32,6,1024]{2,1,0:T(8,128)(2,1)}), bf16[32,6,1024]{2,1,0:T(8,128)(2,1)}, u32[]{:S(2)}, u32[]{:S(2)}) async-start(bf16[32,6,1024]{2,1,0:T(8,128)(2,1)} %reshape.104), calls=%async_computation.1 | async-start | bytes 1048576 | tf_op jit(solution)/shard_map/all_to_all | solution.py:123
  37.7 99.5 %all-gather.8.cloned.1.call-start = ((), (), s32[]{:S(2)}) async-start(), calls=%async_computation.5 | async-start | bytes 2162688 | tf_op jit(solution)/shard_map/all_gather | solution.py:156
  56.1 0.7 copy-start.5
  56.8 2.7 copy-start.8
  58.1 139.2 %all-gather.10.cloned.1.call-start = ((), (), s32[]{:S(2)}) async-start(), calls=%async_computation.6 | async-start | bytes 2162688 | tf_op jit(solution)/shard_map/all_gather | solution.py:157
  58.8 236.5 %all-gather.12.cloned.1.call-start = ((), (), s32[]{:S(2)}) async-start(), calls=%async_computation.7 | async-start | bytes 2162688 | tf_op jit(solution)/shard_map/all_gather | solution.py:187
  59.4 364.0 %reduce-scatter.5.cloned.1.call-start = ((), (), s32[]{:S(2)}) async-start(), calls=%async_computation.8 | async-start | bytes 3244032 | tf_op jit(solution)/shard_map/reduce_scatter | solution.py:200
  203.6 4.8 copy-start.1
  203.6 3.1 copy-start.4
  203.6 3.1 copy-start.9
  299.3 2.4 copy-start.3
  301.8 2.0 copy-start.2
  303.8 12.7 %copy-start.6 = (bf16[64,1024]{1,0:T(8,128)(2,1)S(1)}, bf16[64,1024]{1,0:T(8,128)(2,1)}, u32[]{:S(2)}) copy-start(bf16[64,1024]{1,0:T(8,128)(2,1)} %copy-done.5) | copy-start | bytes 393220
  316.5 2.7 copy-start.7
  319.2 13.4 %copy-start.11 = (f32[192]{0:T(256)S(1)}, f32[192]{0:T(256)}, u32[]{:S(2)}) copy-start(f32[192]{0:T(256)} %copy-done.10) | copy-start | bytes 2308
  319.2 13.4 %copy-start.14 = (s32[1,196]{1,0:T(1,128)S(1)}, s32[1,196]{1,0:T(1,128)}, u32[]{:S(2)}) copy-start(s32[1,196]{1,0:T(1,128)} %param.7) | copy-start | bytes 2356
  319.2 106.0 %copy-start.13 = (s32[1,192]{1,0:T(1,128)S(1)}, s32[1,192]{1,0:T(1,128)}, u32[]{:S(2)}) copy-start(s32[1,192]{1,0:T(1,128)} %copy-done.12) | copy-start | bytes 2308
  322.3 25.7 %all-to-all-start.2 = ((bf16[32,6,1024]{2,1,0:T(8,128)(2,1)}), bf16[32,6,1024]{2,1,0:T(8,128)(2,1)}, u32[]{:S(2)}, u32[]{:S(2)}) async-start(bf16[32,6,1024]{2,1,0:T(8,128)(2,1)} %reshape.116), calls=%async_computation.2 | async-start | bytes 1048576 | tf_op jit(solution)/shard_map/all_to_all | solution.py:209
  332.6 166.7 %reduce-scatter.7.cloned.1.call-start = ((), (), s32[]{:S(2)}) async-start(), calls=%async_computation.10 | async-start | bytes 417792
Sparse Core Ops, SparseCore 0:
  11.1 66.1 all-gather.13
  80.4 56.8 all-gather.7
  140.4 56.8 all-gather.9
  200.8 56.8 all-gather.11
  319.3 104.0 reduce-scatter.4
  426.1 73.1 reduce-scatter.6
where the time goes:
time: 509 us; the launch traced here: 508 us
  waiting for transfers between devices  308 us (61%)
  blocking collectives  79.2 us (16%)
  local copies, waits for them, and re-layouts  43.7 us (9%)
  matrix products  27.9 us (5%)
  starting transfers between devices  26.4 us (5%)
  between operations  14.4 us (3%)
  other arithmetic  8.04 us (2%)
    unnamed x7, waiting for transfers between devices  74.7 us
    reduce_scatter x1, waiting for transfers between devices, local(): lax.psum_scatter(partial_value, 'seq', scatter_dimension=0, tiled=True)  74.2 us
    all_gather x1, waiting for transfers between devices, local(): lax.all_gather(value_rows, 'seq', axis=0, tiled=True)  56.1 us
    all_gather x1, waiting for transfers between devices, local(): lax.all_gather(key_rows, 'seq', axis=0, tiled=True)  56 us
    all_gather x1, blocking collectives, local(): lax.all_gather(log_total.T, 'seq', axis=0, tiled=True)  40.2 us
    all_gather x1, blocking collectives, local(): lax.all_gather(grad_dot, 'seq', axis=0, tiled=True)  38.9 us
    all_to_all x1, waiting for transfers between devices, local(): lax.all_to_all(send_rows.reshape(shard_count, pair_cap, -1), 'seq', split...  15.6 us
    all_to_all x1, waiting for transfers between devices, local(): lax.all_to_all(back_rows.reshape(shard_count, pair_cap, -1), 'seq', split...  13.7 us
  transfers between devices with their start and end apart: 9, of which 8 were waited for; matrix products, arithmetic and copies ran while one was open for 10% of the time, Pallas kernels for 0%

commit v1 on v0

--- a/solution.py
+++ b/solution.py
@@ -6,6 +6,13 @@
 HEADS = 8
 HEAD_DIM = 64
 neg_large = -1e30
+
+
+def gather_over(shard, mesh_axis, dim):
+    n_dev = lax.axis_size(mesh_axis)
+    pieces = jnp.stack([shard for _ in range(n_dev)])
+    pieces = lax.all_to_all(pieces, mesh_axis, split_axis=0, concat_axis=0)
+    return jnp.concatenate(pieces, axis=dim)
 
 
 def split_heads(rows_in):
@@ -176,7 +183,7 @@
     )
     all_log, all_dot = (
         lax.all_gather(log_total.T, "seq", axis=0, tiled=True),
-        lax.all_gather(grad_dot, "seq", axis=0, tiled=True),
+        gather_over(grad_dot, "seq", 0),
     )
     key_grad, value_grad = key_fold(
         split_heads(key_rows),

time: 509 us -> 481 us (0.945)
  blocking collectives: 79.2 us -> 40.2 us
  starting transfers between devices: 26.4 us -> 33.4 us
    all_gather x1 -> x0, blocking collectives: 38.9 us -> none  [local(): lax.all_gather(grad_dot, 'seq', axis=0, tiled=True)]
    all_to_all x0 -> x1, starting transfers between devices: none -> 7.18 us  [gather_over(): pieces = lax.all_to_all(pieces, mesh_axis, split_axis=0, concat_axis=0)]
    unnamed x38 -> x42, local copies, waits for them, and re-layouts: 10.2 us -> 12.7 us
  transfers between devices with their start and end apart: 9 -> 10, of which waited for: 8 -> 8; matrix products, arithmetic and copies ran while one was open for 10% -> 12% of each run, Pallas kernels for 0% -> 0%
where the time goes in v1:
time: 481 us; the launch traced here: 479 us
  waiting for transfers between devices  307 us (64%)
  local copies, waits for them, and re-layouts  46.6 us (10%)
  blocking collectives  40.2 us (8%)
  starting transfers between devices  33.4 us (7%)
  matrix products  27.5 us (6%)
  between operations  14.4 us (3%)
  other arithmetic  9.69 us (2%)
    unnamed x7, waiting for transfers between devices  74.9 us
    reduce_scatter x1, waiting for transfers between devices, local(): lax.psum_scatter(partial_value, 'seq', scatter_dimension=0, tiled=True)  73 us
    all_gather x1, waiting for transfers between devices, local(): lax.all_gather(key_rows, 'seq', axis=0, tiled=True)  56.3 us
    all_gather x1, waiting for transfers between devices, local(): lax.all_gather(value_rows, 'seq', axis=0, tiled=True)  56 us
    all_gather x1, blocking collectives, local(): lax.all_gather(log_total.T, 'seq', axis=0, tiled=True)  40.2 us
    all_to_all x1, waiting for transfers between devices, local(): lax.all_to_all(send_rows.reshape(shard_count, pair_cap, -1), 'seq', split...  15.7 us
    all_to_all x1, waiting for transfers between devices, local(): lax.all_to_all(back_rows.reshape(shard_count, pair_cap, -1), 'seq', split...  13.9 us
    all_gather x1, waiting for transfers between devices, local(): lax.all_gather(grad_rows, 'seq', axis=0, tiled=True)  13.5 us
  transfers between devices with their start and end apart: 10, of which 8 were waited for; matrix products, arithmetic and copies ran while one was open for 12% of the time, Pallas kernels for 0%

profile of v1, /device:TPU:2, one launch (start us, length us, event | category | flops | bytes accessed | tf_op | source)
XLA Modules:
  0.0 479.3 jit_solution(8494886509361190464)
XLA Ops:
  13.2 10.3 %all-to-all-start = ((s32[32,1,6]{2,1,0:T(1,128)}), s32[32,1,6]{2,1,0:T(1,128)S(1)}, u32[]{:S(2)}, u32[]{:S(2)}) async-start(s32[32,1,6]{2,1,0:T(1,128)} %bitcast.5), calls=%async_computation | async-start | bytes 32768 | tf_op jit(solution)/shard_map/all_to_all | solution.py:137
  27.8 4.2 all-to-all-done
  32.0 5.7 %all-to-all-start.1 = ((bf16[32,6,1024]{2,1,0:T(8,128)(2,1)}), bf16[32,6,1024]{2,1,0:T(8,128)(2,1)}, u32[]{:S(2)}, u32[]{:S(2)}) async-start(bf16[32,6,1024]{2,1,0:T(8,128)(2,1)} %reshape.109), calls=%async_computation.1 | async-start | bytes 1048576 | tf_op jit(solution)/shard_map/all_to_all | solution.py:130
  39.0 15.7 %all-to-all-done.1 = bf16[32,6,1024]{2,1,0:T(8,128)(2,1)} async-done(((bf16[32,6,1024]{2,1,0:T(8,128)(2,1)}), bf16[32,6,1024]{2,1,0:T(8,128)(2,1)}, u32[]{:S(2)}, u32[]{:S(2)}) %all-to-all-start.1) | async-done | bytes 393248 | tf_op jit(solution)/shard_map/all_to_all | solution.py:130
  63.7 13.5 %all-gather.13.cloned.1.call-done = bf16[1,2048,512]{2,1,0:T(8,128)(2,1)} async-done(((bf16[1,64,512]{2,1,0:T(8,128)(2,1)}), bf16[1,2048,512]{2,1,0:T(8,128)(2,1)}) %all-gather.13.cloned.1.call-update) | async-done | bytes 2097168 | tf_op jit(solution)/shard_map/all_gather | solution.py:195
  77.2 3.9 copy.79
  81.2 56.3 %all-gather.7.cloned.1.call-done = bf16[2048,512]{1,0:T(8,128)(2,1)} async-done(((bf16[64,512]{1,0:T(8,128)(2,1)}), bf16[2048,512]{1,0:T(8,128)(2,1)}) %all-gather.7.cloned.1.call-update) | async-done | bytes 2097168 | tf_op jit(solution)/shard_map/all_gather | solution.py:163
  137.5 4.0 copy.70
  141.4 56.0 %all-gather.9.cloned.1.call-done = bf16[2048,512]{1,0:T(8,128)(2,1)} async-done(((bf16[64,512]{1,0:T(8,128)(2,1)}), bf16[2048,512]{1,0:T(8,128)(2,1)}) %all-gather.9.cloned.1.call-update) | async-done | bytes 2097168 | tf_op jit(solution)/shard_map/all_gather | solution.py:164
  197.5 3.9 copy.72
  201.4 2.4 multiply_reduce_fusion
  204.6 2.2 copy-done.4
  209.3 7.2 %all-to-all-start.2 = ((f32[32,1,512]{2,1,0:T(1,128)}), f32[32,1,512]{2,1,0:T(1,128)}, u32[]{:S(2)}, u32[]{:S(2)}) async-start(f32[32,1,512]{2,1,0:T(1,128)} %reshape.141), calls=%async_computation.2 | async-start | bytes 131072 | tf_op jit(solution)/shard_map/all_to_all | solution.py:14
  216.5 40.2 %all-gather.1 = f32[32,64,8]{1,2,0:T(8,128)S(1)} all-gather(f32[1,64,8]{1,2,0:T(8,128)S(1)} %fusion.58), channel_id=1, replica_groups=mesh['clip'=16,'seq'=32] {'seq'}, dimensions={0}, use_global_device_ids=true | all-gather | bytes 67584 | tf_op jit(solution)/shard_map/all_gather | solution.py:185
  256.8 5.9 %fusion.28 = bf16[64,8,64]{2,0,1:T(8,128)(2,1)} fusion(bf16[2048,8,64]{0,2,1:T(8,128)(2,1)} %bitcast.108, f32[8,64,2048]{2,1,0:T(8,128)} %copy-done.2, bf16[2048,8,64]{0,2,1:T(8,128)(2,1)} %bitcast.109, bf16[64,8,64]{0,2,1:T(8,128)(2,1)} %bitcast.116, f32[8,64]{1,0:T(8,128)S(1)} %bitcast.123, f32[8,64]{1,0:T(8,128)S(1)} %log_add_fusion), kind=kOutput, calls=%fused_computation.36 | convolution fusion | flops 273743872 | bytes 8523776 | tf_op jit(solution)/shard_map/hrk,khd->hrd/dot_general | solution.py:59
  262.8 4.0 copy.76
  266.8 2.4 fusion.44
  274.2 2.3 reduce.6
  279.7 5.9 %fusion.29 = bf16[64,8,64]{2,0,1:T(8,128)(2,1)} fusion(bf16[2048,8,64]{0,2,1:T(8,128)(2,1)} %bitcast.106, f32[8,2048,64]{1,2,0:T(8,128)} %copy-done.1, bf16[2048,8,64]{0,2,1:T(8,128)(2,1)} %bitcast.103, f32[8,2048]{1,0:T(8,128)} %bitcast.118, f32[8,2048]{1,0:T(8,128)S(1)} %bitcast.114, bf16[64,8,64]{2,1,0:T(8,128)(2,1)} %reshape.117), kind=kOutput, calls=%fused_computation.37 | convolution fusion | flops 273743872 | bytes 8650752 | tf_op jit(solution)/shard_map/hqk,qhd->hkd/dot_general | solution.py:88
  289.1 2.6 convolution_convert_fusion
  295.0 10.1 %all-to-all-start.3 = ((bf16[32,6,1024]{2,1,0:T(8,128)(2,1)}), bf16[32,6,1024]{2,1,0:T(8,128)(2,1)}, u32[]{:S(2)}, u32[]{:S(2)}) async-start(bf16[32,6,1024]{2,1,0:T(8,128)(2,1)} %reshape.122), calls=%async_computation.3 | async-start | bytes 1048576 | tf_op jit(solution)/shard_map/all_to_all | solution.py:216
  306.8 13.9 %all-to-all-done.3 = bf16[32,6,1024]{2,1,0:T(8,128)(2,1)} async-done(((bf16[32,6,1024]{2,1,0:T(8,128)(2,1)}), bf16[32,6,1024]{2,1,0:T(8,128)(2,1)}, u32[]{:S(2)}, u32[]{:S(2)}) %all-to-all-start.3) | async-done | bytes 393248 | tf_op jit(solution)/shard_map/all_to_all | solution.py:216
  321.9 73.0 %reduce-scatter.5.cloned.1.call-done = bf16[32,1536]{1,0:T(8,128)(2,1)} async-done(((bf16[1024,1536]{1,0:T(8,128)(2,1)}), bf16[32,1536]{1,0:T(8,128)(2,1)}) %reduce-scatter.5.cloned.1.call-update) | async-done | bytes 98320 | tf_op jit(solution)/shard_map/reduce_scatter | solution.py:207
  398.0 72.9 %reduce-scatter.7.cloned.1.call-done = bf16[96,32]{1,0:T(8,128)(2,1)} async-done(((bf16[1536,32]{1,0:T(8,128)(2,1)}), bf16[96,32]{1,0:T(8,128)(2,1)}) %reduce-scatter.7.cloned.1.call-update) | async-done | bytes 6160
  (105 shorter events, 46.4 us)
Async XLA Ops:
  7.2 49.5 %copy-start = (bf16[1024,1536]{1,0:T(8,128)(2,1)S(1)}, bf16[1024,1536]{1,0:T(8,128)(2,1)}, u32[]{:S(2)}) copy-start(bf16[1024,1536]{1,0:T(8,128)(2,1)} %param.10) | copy-start | bytes 9437188
  7.2 70.1 %all-gather.13.cloned.1.call-start = ((), (), s32[]{:S(2)}) async-start(), calls=%async_computation.10 | async-start | bytes 2162688 | tf_op jit(solution)/shard_map/all_gather | solution.py:195
  13.2 18.8 %all-to-all-start = ((s32[32,1,6]{2,1,0:T(1,128)}), s32[32,1,6]{2,1,0:T(1,128)S(1)}, u32[]{:S(2)}, u32[]{:S(2)}) async-start(s32[32,1,6]{2,1,0:T(1,128)} %bitcast.5), calls=%async_computation | async-start | bytes 32768 | tf_op jit(solution)/shard_map/all_to_all | solution.py:137
  32.0 22.7 %all-to-all-start.1 = ((bf16[32,6,1024]{2,1,0:T(8,128)(2,1)}), bf16[32,6,1024]{2,1,0:T(8,128)(2,1)}, u32[]{:S(2)}, u32[]{:S(2)}) async-start(bf16[32,6,1024]{2,1,0:T(8,128)(2,1)} %reshape.109), calls=%async_computation.1 | async-start | bytes 1048576 | tf_op jit(solution)/shard_map/all_to_all | solution.py:130
  37.6 99.8 %all-gather.7.cloned.1.call-start = ((), (), s32[]{:S(2)}) async-start(), calls=%async_computation.6 | async-start | bytes 2162688 | tf_op jit(solution)/shard_map/all_gather | solution.py:163
  56.0 0.7 copy-start.5
  56.7 2.7 copy-start.8
  58.1 139.4 %all-gather.9.cloned.1.call-start = ((), (), s32[]{:S(2)}) async-start(), calls=%async_computation.7 | async-start | bytes 2162688 | tf_op jit(solution)/shard_map/all_gather | solution.py:164
  58.8 204.0 %all-gather.11.cloned.1.call-start = ((), (), s32[]{:S(2)}) async-start(), calls=%async_computation.8 | async-start | bytes 2162688 | tf_op jit(solution)/shard_map/all_gather | solution.py:194
  203.8 4.8 copy-start.2
  203.8 3.1 copy-start.4
  203.8 3.1 copy-start.9
  209.3 64.4 %all-to-all-start.2 = ((f32[32,1,512]{2,1,0:T(1,128)}), f32[32,1,512]{2,1,0:T(1,128)}, u32[]{:S(2)}, u32[]{:S(2)}) async-start(f32[32,1,512]{2,1,0:T(1,128)} %reshape.141), calls=%async_computation.2 | async-start | bytes 131072 | tf_op jit(solution)/shard_map/all_to_all | solution.py:14
  216.5 178.4 %reduce-scatter.5.cloned.1.call-start = ((), (), s32[]{:S(2)}) async-start(), calls=%async_computation.9 | async-start | bytes 3244032 | tf_op jit(solution)/shard_map/reduce_scatter | solution.py:207
  266.8 2.4 copy-start.3
  269.2 1.9 copy-start.1
  269.2 1.9 copy-start.10
  279.7 9.4 %copy-start.6 = (bf16[64,1024]{1,0:T(8,128)(2,1)S(1)}, bf16[64,1024]{1,0:T(8,128)(2,1)}, u32[]{:S(2)}) copy-start(bf16[64,1024]{1,0:T(8,128)(2,1)} %copy-done.5) | copy-start | bytes 393220
  289.1 2.7 copy-start.7
  291.8 13.3 %copy-start.12 = (f32[192]{0:T(256)S(1)}, f32[192]{0:T(256)}, u32[]{:S(2)}) copy-start(f32[192]{0:T(256)} %copy-done.11) | copy-start | bytes 2308
  291.8 13.3 %copy-start.15 = (s32[1,196]{1,0:T(1,128)S(1)}, s32[1,196]{1,0:T(1,128)}, u32[]{:S(2)}) copy-start(s32[1,196]{1,0:T(1,128)} %param.7) | copy-start | bytes 2356
  291.8 104.9 %copy-start.14 = (s32[1,192]{1,0:T(1,128)S(1)}, s32[1,192]{1,0:T(1,128)}, u32[]{:S(2)}) copy-start(s32[1,192]{1,0:T(1,128)} %copy-done.13) | copy-start | bytes 2308
  295.0 25.8 %all-to-all-start.3 = ((bf16[32,6,1024]{2,1,0:T(8,128)(2,1)}), bf16[32,6,1024]{2,1,0:T(8,128)(2,1)}, u32[]{:S(2)}, u32[]{:S(2)}) async-start(bf16[32,6,1024]{2,1,0:T(8,128)(2,1)} %reshape.122), calls=%async_computation.3 | async-start | bytes 1048576 | tf_op jit(solution)/shard_map/all_to_all | solution.py:216
  305.0 165.9 %reduce-scatter.7.cloned.1.call-start = ((), (), s32[]{:S(2)}) async-start(), calls=%async_computation.11 | async-start | bytes 417792
  (2 other events, 1.1 us)
Sparse Core Ops, SparseCore 0:
  11.1 66.0 all-gather.12
  80.4 57.0 all-gather.6
  140.6 56.8 all-gather.8
  201.0 57.0 all-gather.10
  291.9 102.9 reduce-scatter.4
  397.6 73.3 reduce-scatter.6
